TPU v7x, 128 devices: a whole 4x4x4 slice. The times are simulated.
128 devices in a mesh: qx: 8 (over y, core), qy: 16 (over x, z).
Axes of the slice: x: 4, y: 4, z: 4, core: 2. Of those that a mesh axis runs over, the one named last changes fastest.
Arguments:
- positions: float32 [32, 64, 2, 256], replicated, may hold values from 0 to 64, as said below
- samples: bfloat16 [32, 64, 256, 256], P('qx', 'qy'), may hold values from -6 to 6
- leaf_basis: bfloat16 [32, 64, 256, 256], P('qx', 'qy'), may hold values from -0.375 to 0.375
- transfer_one: bfloat16 [32, 64, 256, 256], P('qx', 'qy'), may hold values from -0.25 to 0.25
- transfer_two: bfloat16 [16, 32, 256, 256], P('qx', 'qy'), may hold values from -0.25 to 0.25
- couplings: bfloat16 [3, 20, 256, 256], replicated, may hold values from -0.078125 to 0.078125
- near_lists: int32 [32, 64, 9], P('qx', 'qy'), may hold values from -1 to 2047, as said below
- far_zero: int32 [32, 64, 27], P('qx', 'qy'), may hold values from -1 to 2047, as said below
- far_one: int32 [16, 32, 27], P('qx', 'qy'), may hold values from -1 to 511, as said below
- far_two: int32 [8, 16, 27], P('qx', 'qy'), may hold values from -1 to 127, as said below
Outputs:
- product: bfloat16 [32, 64, 256, 256], P('qx', 'qy')
Inputs may be any that keep to these rules, and one draw needn't show every extreme that they name: Site p of leaf (i, j) lies at positions[i, j, 0, p] between i and i + 1 and positions[i, j, 1, p] between j and j + 1. `near_lists`: every entry of the list of leaf (i, j) is -1 or the id r * 64 + c of a leaf (r, c) with abs(r - i) <= 1 and abs(c - j) <= 1; the leaf's own id is always in its list, and no id stands twice. `far_zero`: every entry of the list of leaf (i, j) is -1 or the id r * 64 + c of a leaf (r, c) with max(abs(r - i), abs(c - j)) >= 2 whose parent (r // 2, c // 2) is within one step of (i // 2, j // 2) along each coordinate; no id stands twice. `far_one`: every entry of the list of level-1 cell (i, j) is -1 or the id r * 32 + c of a level-1 cell (r, c) with max(abs(r - i), abs(c - j)) >= 2 and (r // 2, c // 2) within one step of (i // 2, j // 2) along each coordinate; no id stands twice. `far_two`: every entry of the list of level-2 cell (i, j) is -1 or the id r * 16 + c of a level-2 cell (r, c) with max(abs(r - i), abs(c - j)) >= 2 and (r // 2, c // 2) within one step of (i // 2, j // 2) along each coordinate; no id stands twice.
All inputs are finite; a program needn't handle non-finite values.
Results may differ from a plain program's by a relative error of at most 0.0085.
Values may be sent and summed in bfloat16 or wider, within the bound.
A program may use at most 256 MiB of HBM per device.

v0:
```python
import jax
import jax.numpy as jnp
import numpy as np
from jax import lax
from jax.sharding import PartitionSpec as P

root_three = 1.7320508075688772
length_scale = 1.0


def padded(block, sides, width):
    for axis, dim in sides:
        count = lax.axis_size(axis)
        forward = [(i, i + 1) for i in range(count - 1)]
        backward = [(target, source) for source, target in forward]
        low = lax.ppermute(
            lax.slice_in_dim(block, block.shape[dim] - width, None, axis=dim), axis, forward
        )
        high = lax.ppermute(lax.slice_in_dim(block, 0, width, axis=dim), axis, backward)
        block = jnp.concatenate([low, block, high], axis=dim)
    return block


def passed_along(x, axis, by):
    peers = lax.axis_size(axis)
    pairs = [(i, i + by) for i in range(peers) if 0 <= i + by < peers]
    return lax.ppermute(x, axis, pairs)


def offset_plan():
    slot_of = np.zeros((49,), np.int32)
    flip_of = np.zeros((49,), np.int32)
    active = np.zeros((49,), np.int32)
    upper_half = []
    for number in range(49):
        row_step = number // 7 - 3
        col_step = number % 7 - 3
        if max(abs(row_step), abs(col_step)) >= 2 and (
            row_step > 0 or (row_step == 0 and col_step > 0)
        ):
            upper_half.append(number)
    for number in range(49):
        row_step = number // 7 - 3
        col_step = number % 7 - 3
        if max(abs(row_step), abs(col_step)) >= 2:
            active[number] = 1
            if number in upper_half:
                slot_of[number] = upper_half.index(number)
            else:
                slot_of[number] = upper_half.index((3 - row_step) * 7 + 3 - col_step)
                flip_of[number] = 1
    return (slot_of, flip_of, active)


def coupling_table(level_couplings):
    slot_of, flip_of, active = offset_plan()
    pieces = []
    for number in range(49):
        matrix = level_couplings[int(slot_of[number])]
        if flip_of[number] == 1:
            matrix = matrix.T
        if active[number] == 0:
            matrix = jnp.zeros_like(matrix)
        pieces.append(matrix)
    return jnp.stack(pieces)


def matern_tiles(targets, sources, allowed):
    gap_rows = targets[:, 0][:, :, None] - sources[:, 0][:, None, :]
    gap_cols = targets[:, 1][:, :, None] - sources[:, 1][:, None, :]
    distance = jnp.sqrt(gap_rows * gap_rows + gap_cols * gap_cols)
    scaled = root_three * distance / length_scale
    variance = float(sources.shape[2]) ** (-0.5)
    kernel_value = (1.0 + scaled) * jnp.exp(-scaled) * variance
    return jnp.where(allowed[:, None, None], kernel_value, 0.0).astype(jnp.bfloat16)


def children_sum(transfer, coef):
    child_terms = jnp.einsum("xyrs,xyrc->xysc", transfer, coef, preferred_element_type=jnp.float32)
    grid_rows, grid_cols = (coef.shape[0], coef.shape[1])
    shaped = child_terms.reshape(
        grid_rows // 2, 2, grid_cols // 2, 2, transfer.shape[3], coef.shape[3]
    )
    return shaped.sum(axis=(1, 3))


def descend(transfer, parent):
    grid_rows, grid_cols = (parent.shape[0], parent.shape[1])
    shaped = transfer.reshape(grid_rows, 2, grid_cols, 2, transfer.shape[2], transfer.shape[3])
    spread = jnp.einsum("xaybrs,xysc->xaybrc", shaped, parent, preferred_element_type=jnp.float32)
    return spread.reshape(2 * grid_rows, 2 * grid_cols, transfer.shape[2], parent.shape[3])


def far_block(extended, lists, couple_table, first_row, first_col, ext_row, ext_col, grid_cols):
    block_rows, block_cols, slot_count = lists.shape
    ext_cols = extended.shape[1]
    flattened = extended.reshape(-1, extended.shape[2], extended.shape[3])
    source_ids = lists.reshape(block_rows * block_cols, slot_count)
    usable = source_ids >= 0
    clipped = jnp.maximum(source_ids, 0)
    source_row = clipped // grid_cols
    source_col = clipped % grid_cols
    cell_ids = jnp.arange(block_rows * block_cols, dtype=jnp.int32)
    target_row = first_row + (cell_ids // block_cols)[:, None]
    target_col = first_col + (cell_ids % block_cols)[:, None]
    offset_kind = jnp.clip((source_row - target_row + 3) * 7 + source_col - target_col + 3, 0, 48)
    located = jnp.clip(
        (source_row - ext_row) * ext_cols + source_col - ext_col, 0, flattened.shape[0] - 1
    )

    def one_cell(packed):
        places, kind_here, allowed = packed
        matrices = jnp.where(
            allowed[:, None, None], couple_table[kind_here], jnp.zeros((), couple_table.dtype)
        )
        return jnp.einsum(
            "jrs,jsc->rc", matrices, flattened[places], preferred_element_type=jnp.float32
        )

    result = lax.map(one_cell, (located, offset_kind, usable))
    return result.reshape(block_rows, block_cols, flattened.shape[1], flattened.shape[2])


def near_prepare(ext_samples, lists, positions, first_row, first_col, grid_cols):
    side_rows, side_cols, slot_count = lists.shape
    ext_cols = ext_samples.shape[1]
    flattened = ext_samples.reshape(-1, ext_samples.shape[2], ext_samples.shape[3])
    source_ids = lists.reshape(-1, slot_count)
    usable = source_ids >= 0
    clipped = jnp.maximum(source_ids, 0)
    located = (
        (clipped // grid_cols - first_row + 1) * ext_cols + clipped % grid_cols - first_col + 1
    )
    located = jnp.clip(located, 0, flattened.shape[0] - 1)
    site_count = positions.shape[3]
    sources = positions.reshape(-1, 2, site_count)[clipped]
    targets = lax.dynamic_slice(
        positions, (first_row, first_col, 0, 0), (side_rows, side_cols, 2, site_count)
    )
    return (flattened, located, usable, sources, targets.reshape(-1, 2, site_count))


def near_padded(flattened, located, usable, sources, targets):

    def one_leaf(packed):
        target, source_rows, places, allowed = packed
        kernel_tiles = matern_tiles(target[None], source_rows, allowed)
        return jnp.einsum(
            "jpq,jqc->pc", kernel_tiles, flattened[places], preferred_element_type=jnp.float32
        )

    return lax.map(one_leaf, (targets, sources, located, usable))


def per_device(
    positions,
    samples,
    leaf_basis,
    transfer_one,
    transfer_two,
    couplings,
    near_lists,
    far_zero,
    far_one,
    far_two,
):
    row_index = lax.axis_index("qx")
    col_index = lax.axis_index("qy")
    col_count = lax.axis_size("qy")
    leaf_side = samples.shape[0]
    half_side = leaf_side // 2
    leaf_cols = leaf_side * col_count
    first_row = row_index * leaf_side
    first_col = col_index * leaf_side
    ext_samples = padded(samples, (("qx", 0), ("qy", 1)), 1)
    coef_zero = jnp.einsum(
        "xypr,xypc->xyrc", leaf_basis, samples, preferred_element_type=jnp.float32
    ).astype(jnp.bfloat16)
    ext_zero = padded(coef_zero, (("qx", 0), ("qy", 1)), 2)
    coef_one = children_sum(transfer_one, coef_zero).astype(jnp.bfloat16)
    ext_one = padded(coef_one, (("qx", 0), ("qy", 1)), 2)
    coef_two = children_sum(transfer_two, coef_one).astype(jnp.bfloat16)
    center = coef_two[0, 0]
    column_list = []
    for offset in range(-3, 4):
        if offset == 0:
            column_list.append(center)
        else:
            column_list.append(passed_along(center, "qx", -offset))
    stacked = jnp.stack(column_list)
    row_list = []
    for offset in range(-3, 4):
        if offset == 0:
            row_list.append(stacked)
        else:
            row_list.append(passed_along(stacked, "qy", -offset))
    block_two = jnp.stack(row_list, axis=1)
    field_two = far_block(
        block_two,
        far_two,
        coupling_table(couplings[2]),
        row_index,
        col_index,
        row_index - 3,
        col_index - 3,
        col_count,
    )
    upper_row = row_index * half_side
    upper_col = col_index * half_side
    field_one = far_block(
        ext_one,
        far_one,
        coupling_table(couplings[1]),
        upper_row,
        upper_col,
        upper_row - 2,
        upper_col - 2,
        leaf_cols // 2,
    )
    field_zero = far_block(
        ext_zero,
        far_zero,
        coupling_table(couplings[0]),
        first_row,
        first_col,
        first_row - 2,
        first_col - 2,
        leaf_cols,
    )
    down_two = field_two.astype(jnp.bfloat16)
    down_one = (field_one + descend(transfer_two, down_two)).astype(jnp.bfloat16)
    down_zero = (field_zero + descend(transfer_one, down_one)).astype(jnp.bfloat16)
    flattened, located, usable, sources, targets = near_prepare(
        ext_samples, near_lists, positions, first_row, first_col, leaf_cols
    )
    near_field = near_padded(flattened, located, usable, sources, targets)
    near_field = near_field.reshape(samples.shape)
    total_sum = near_field + jnp.einsum(
        "xypr,xyrc->xypc", leaf_basis, down_zero, preferred_element_type=jnp.float32
    )
    return total_sum.astype(jnp.bfloat16)


def solution(mesh):
    return jax.shard_map(
        per_device,
        mesh=mesh,
        in_specs=(
            P(),
            P("qx", "qy", None, None),
            P("qx", "qy", None, None),
            P("qx", "qy", None, None),
            P("qx", "qy", None, None),
            P(),
            P("qx", "qy", None),
            P("qx", "qy", None),
            P("qx", "qy", None),
            P("qx", "qy", None),
        ),
        out_specs=P("qx", "qy", None, None),
        check_vma=False,
    )
```

profile of v0, /device:TPU:116, one launch (start us, length us, event | category | flops | bytes accessed | tf_op | source)
XLA Modules:
  0.0 994.2 jit_solution(11522671146459932417)
XLA Ops:
  276.7 5.4 gather_fusion.6
  323.4 26.4 %collective-permute-done.18 = bf16[7,256,256]{1,2,0:T(8,128)(2,1)S(1)} collective-permute-done((bf16[7,256,256]{1,2,0:T(8,128)(2,1)S(1)}, bf16[7,256,256]{1,2,0:T(8,128)(2,1)S(1)}, u32[]{:S(2)}, u32[]{:S(2)}) %collective-permute-start.18) | collective-permute-done | bytes 917536 | tf_op jit(solution)/shard_map/ppermute | solution.py:27
  356.5 17.7 %collective-permute-done.20 = bf16[7,256,256]{1,2,0:T(8,128)(2,1)S(1)} collective-permute-done((bf16[7,256,256]{1,2,0:T(8,128)(2,1)S(1)}, bf16[7,256,256]{1,2,0:T(8,128)(2,1)S(1)}, u32[]{:S(2)}, u32[]{:S(2)}) %collective-permute-start.20) | collective-permute-done | bytes 917536 | tf_op jit(solution)/shard_map/ppermute | solution.py:27
  379.2 16.6 %collective-permute-done.21 = bf16[7,256,256]{1,2,0:T(8,128)(2,1)S(1)} collective-permute-done((bf16[7,256,256]{1,2,0:T(8,128)(2,1)S(1)}, bf16[7,256,256]{1,2,0:T(8,128)(2,1)S(1)}, u32[]{:S(2)}, u32[]{:S(2)}) %collective-permute-start.21) | collective-permute-done | bytes 917536 | tf_op jit(solution)/shard_map/ppermute | solution.py:27
  398.8 34.0 %collective-permute-start.11 = (bf16[6,2,256,256]{2,3,1,0:T(8,128)(2,1)}, bf16[6,2,256,256]{2,3,1,0:T(8,128)(2,1)}, u32[]{:S(2)}, u32[]{:S(2)}) collective-permute-start(bf16[6,2,256,256]{2,3,1,0:T(8,128)(2,1)} %pad_maximum_fusion.4), channel_id=1, source_target_pairs={{1,0},{2,1},{3,2},{4,3},{5,4},{6,5},{7,6},{8,7},{9,8},{10,9},{11,1... | collective-permute-start | bytes 4718600 | tf_op jit(solution)/shard_map/ppermute | solution.py:19
  433.8 6.7 collective-permute-done.23
  440.5 9.7 collective-permute-start.2
  451.1 10.9 %copy.145 = bf16[7,7,256,256]{3,2,1,0:T(8,128)(2,1)} copy(bf16[7,7,256,256]{2,3,0,1:T(8,128)(2,1)} %bitcast_dynamic-update-slice_fusion) | data formatting | bytes 12845056 | tf_op jit(solution)/shard_map/stack | solution.py:197
  468.8 6.0 collective-permute-start.6
  474.8 5.5 gather_fusion.7
  487.0 12.3 %collective-permute-done.3 = bf16[6,1,256,256]{3,2,1,0:T(8,128)(2,1)} collective-permute-done((bf16[6,1,256,256]{3,2,1,0:T(8,128)(2,1)}, bf16[6,1,256,256]{3,2,1,0:T(8,128)(2,1)}, u32[]{:S(2)}, u32[]{:S(2)}) %collective-permute-start.3) | collective-permute-done | bytes 786464 | tf_op jit(solution)/shard_map/ppermute | solution.py:19
  502.7 112.8 %while.34 = (s32[]{:T(128)}, f32[16,256,256]{1,2,0:T(8,128)}, pred[16,9]{1,0:T(8,128)(4,1)}, f32[16,2,256]{2,1,0:T(2,128)S(1)}, f32[16,9,2,256]{3,2,1,0:T(2,128)...) while((s32[]{:T(128)}, f32[16,256,256]{1,2,0:T(8,128)}, ...), condition=%wide.region_1.0_spmd, body=%wide.region_0.0_spmd.sunk | while | flops 309068832 | bytes 3941168 | solution.py:152
  615.5 5.5 pad_maximum_fusion.2
  621.0 6.6 copy.123
  627.7 63.7 %while.36 = (s32[]{:T(128)}, f32[4,256,256]{1,2,0:T(8,128)}, pred[4,27]{1,0:T(4,128)(4,1)S(1)}, s32[4,27]{1,0:T(4,128)S(1)}, bf16[49,256,256]{2,1,0:T(8,128)(2,1...) while((s32[]{:T(128)}, f32[4,256,256]{1,2,0:T(8,128)}, pred[4,27]{1,0:T(4,128)(4,1)S(1)}, ...), condition=%wide.region_6.7_spmd, body=%wide.region_5.6_spmd.sunk | while | flops 907741376 | bytes 21505548 | solution.py:120
  627.7 5.0 gather_fusion.3
  632.7 5.5 gather_fusion.4
  638.2 5.4 fusion.121
  643.6 4.9 gather_fusion.3
  648.6 5.5 gather_fusion.4
  654.1 5.4 fusion.121
  659.5 4.9 gather_fusion.3
  664.5 5.5 gather_fusion.4
  670.0 5.4 fusion.121
  675.4 4.9 gather_fusion.3
  680.4 5.5 gather_fusion.4
  685.9 5.4 fusion.121
  695.4 5.2 copy.147
  700.7 7.3 pad_maximum_fusion
  708.0 274.4 %while.35 = (s32[]{:T(128)}, f32[16,256,256]{2,1,0:T(8,128)}, pred[16,27]{1,0:T(8,128)(4,1)}, s32[16,27]{1,0:T(8,128)S(1)}, bf16[49,256,256]{2,1,0:T(8,128)(2,1)...) while((s32[]{:T(128)}, f32[16,256,256]{2,1,0:T(8,128)}, pred[16,27]{1,0:T(8,128)(4,1)}, ...), condition=%wide.region_3.4_spmd, body=%wide.region_2.3_spmd.sunk | while | flops 907741376 | bytes 21505548 | solution.py:120
  708.0 6.0 gather_fusion.1
  714.0 5.5 gather_fusion.2
  725.2 6.0 gather_fusion.1
  731.2 5.5 gather_fusion.2
  742.3 6.0 gather_fusion.1
  748.3 5.5 gather_fusion.2
  759.5 6.0 gather_fusion.1
  765.5 5.5 gather_fusion.2
  776.6 6.0 gather_fusion.1
  782.6 5.5 gather_fusion.2
  793.7 6.0 gather_fusion.1
  799.8 5.5 gather_fusion.2
  810.9 6.0 gather_fusion.1
  816.9 5.5 gather_fusion.2
  828.0 6.0 gather_fusion.1
  834.0 5.5 gather_fusion.2
  845.2 6.0 gather_fusion.1
  851.2 5.5 gather_fusion.2
  862.3 6.0 gather_fusion.1
  868.3 5.5 gather_fusion.2
  874.5 4.9 fusion.117
  879.5 6.0 gather_fusion.1
  885.5 5.5 gather_fusion.2
  896.7 6.0 gather_fusion.1
  902.7 5.5 gather_fusion.2
  913.8 6.0 gather_fusion.1
  919.8 5.5 gather_fusion.2
  931.0 6.0 gather_fusion.1
  937.0 5.5 gather_fusion.2
  948.2 6.0 gather_fusion.1
  954.2 5.5 gather_fusion.2
  965.3 6.0 gather_fusion.1
  971.3 5.5 gather_fusion.2
  982.4 7.6 fusion.48
  (548 shorter events, 556.6 us)
Async XLA Ops:
  0.0 4.5 copy-start
  3.1 1.3 copy-start.1
  4.5 5.3 copy-start.8
  9.8 303.8 %copy-start.5 = (bf16[2,2,256,256]{2,3,1,0:T(8,128)(2,1)}, bf16[2,2,256,256]{2,3,1,0:T(8,128)(2,1)S(1)}, u32[]{:S(2)}) copy-start(bf16[2,2,256,256]{2,3,1,0:T(8,128)(2,1)S(1)} %reduce_sum.8) | copy-start | bytes 1572868
  10.1 276.1 %collective-permute-start.12 = (bf16[256,256]{0,1:T(8,128)(2,1)S(1)}, bf16[256,256]{0,1:T(8,128)(2,1)}, u32[]{:S(2)}, u32[]{:S(2)}) collective-permute-start(bf16[256,256]{0,1:T(8,128)(2,1)S(1)} %bitcast.742), channel_id=1, source_target_pairs={{0,48},{16,64},{32,80},{48,96},{64,112},{1,49},{17,65},{33,81},{49... | collective-permute-start | bytes 393224 | tf_op jit(solution)/shard_map/ppermute | solution.py:27
  12.8 276.5 %collective-permute-start.13 = (bf16[256,256]{0,1:T(8,128)(2,1)S(1)}, bf16[256,256]{0,1:T(8,128)(2,1)}, u32[]{:S(2)}, u32[]{:S(2)}) collective-permute-start(bf16[256,256]{0,1:T(8,128)(2,1)S(1)} %bitcast.743), channel_id=1, source_target_pairs={{0,32},{16,48},{32,64},{48,80},{64,96},{80,112},{1,33},{17,49},{33... | collective-permute-start | bytes 393224 | tf_op jit(solution)/shard_map/ppermute | solution.py:27
  14.7 277.9 %collective-permute-start.14 = (bf16[256,256]{0,1:T(8,128)(2,1)S(1)}, bf16[256,256]{0,1:T(8,128)(2,1)}, u32[]{:S(2)}, u32[]{:S(2)}) collective-permute-start(bf16[256,256]{0,1:T(8,128)(2,1)S(1)} %bitcast.744), channel_id=1, source_target_pairs={{0,16},{16,32},{32,48},{48,64},{64,80},{80,96},{96,112},{1,17},{17... | collective-permute-start | bytes 393224 | tf_op jit(solution)/shard_map/ppermute | solution.py:27
  16.6 280.1 %collective-permute-start.15 = (bf16[256,256]{0,1:T(8,128)(2,1)S(1)}, bf16[256,256]{0,1:T(8,128)(2,1)}, u32[]{:S(2)}, u32[]{:S(2)}) collective-permute-start(bf16[256,256]{0,1:T(8,128)(2,1)S(1)} %bitcast.745), channel_id=1, source_target_pairs={{16,0},{32,16},{48,32},{64,48},{80,64},{96,80},{112,96},{17,1},{33... | collective-permute-start | bytes 393224 | tf_op jit(solution)/shard_map/ppermute | solution.py:27
  20.3 280.5 %collective-permute-start.16 = (bf16[256,256]{0,1:T(8,128)(2,1)S(1)}, bf16[256,256]{0,1:T(8,128)(2,1)}, u32[]{:S(2)}, u32[]{:S(2)}) collective-permute-start(bf16[256,256]{0,1:T(8,128)(2,1)S(1)} %bitcast.746), channel_id=1, source_target_pairs={{32,0},{48,16},{64,32},{80,48},{96,64},{112,80},{33,1},{49,17},{65... | collective-permute-start | bytes 393224 | tf_op jit(solution)/shard_map/ppermute | solution.py:27
  27.8 8.6 copy-start.14
  27.8 10.4 %copy-start.10 = (s32[4,4,27]{2,1,0:T(4,128)S(1)}, s32[4,4,27]{2,1,0:T(4,128)}, u32[]{:S(2)}) copy-start(s32[4,4,27]{2,1,0:T(4,128)} %param.23) | copy-start | bytes 5188
  228.9 18.1 %copy-start.24 = (pred[2,2,27]{2,1,0:T(4,128)(4,1)S(1)}, pred[2,2,27]{2,1,0:T(4,128)(4,1)}, u32[]{:S(2)}) copy-start(pred[2,2,27]{2,1,0:T(4,128)(4,1)} %get-tuple-element.338) | copy-start | bytes 328
  228.9 18.2 %copy-start.23 = (pred[2,2,27]{2,1,0:T(4,128)(4,1)S(1)}, pred[2,2,27]{2,1,0:T(4,128)(4,1)}, u32[]{:S(2)}) copy-start(pred[2,2,27]{2,1,0:T(4,128)(4,1)} %get-tuple-element.339) | copy-start | bytes 328
  228.9 18.8 %copy-start.13 = (s32[4,4,9]{2,1,0:T(4,128)S(1)}, s32[4,4,9]{2,1,0:T(4,128)}, u32[]{:S(2)}) copy-start(s32[4,4,9]{2,1,0:T(4,128)} %get-tuple-element.335) | copy-start | bytes 1732
  228.9 18.9 %copy-start.25 = (s32[1,1,27]{2,1,0:T(1,128)S(1)}, s32[1,1,27]{2,1,0:T(1,128)}, u32[]{:S(2)}) copy-start(s32[1,1,27]{2,1,0:T(1,128)} %param.25) | copy-start | bytes 328
  264.0 22.0 %copy-start.12 = (s32[4,4,9]{2,1,0:T(4,128)S(1)}, s32[4,4,9]{2,1,0:T(4,128)}, u32[]{:S(2)}) copy-start(s32[4,4,9]{2,1,0:T(4,128)} %get-tuple-element.334) | copy-start | bytes 1732
  264.0 22.0 %copy-start.18 = (pred[4,4,9]{2,1,0:T(4,128)(4,1)S(1)}, pred[4,4,9]{2,1,0:T(4,128)(4,1)}, u32[]{:S(2)}) copy-start(pred[4,4,9]{2,1,0:T(4,128)(4,1)} %get-tuple-element.331) | copy-start | bytes 436
  265.8 20.2 %copy-start.15 = (s32[2,2,27]{2,1,0:T(2,128)S(1)}, s32[2,2,27]{2,1,0:T(2,128)}, u32[]{:S(2)}) copy-start(s32[2,2,27]{2,1,0:T(2,128)} %get-tuple-element.340) | copy-start | bytes 1300
  265.8 20.2 %copy-start.16 = (s32[2,2,27]{2,1,0:T(2,128)S(1)}, s32[2,2,27]{2,1,0:T(2,128)}, u32[]{:S(2)}) copy-start(s32[2,2,27]{2,1,0:T(2,128)} %get-tuple-element.341) | copy-start | bytes 1300
  265.8 20.2 %copy-start.21 = (s32[4]{0:T(128)S(1)}, s32[4]{0:T(128)}, u32[]{:S(2)}) copy-start(s32[4]{0:T(128)} %get-tuple-element.350) | copy-start | bytes 52
  265.8 20.2 %copy-start.22 = (s32[4]{0:T(128)S(1)}, s32[4]{0:T(128)}, u32[]{:S(2)}) copy-start(s32[4]{0:T(128)} %get-tuple-element.351) | copy-start | bytes 52
  265.8 20.3 %copy-start.11 = (s32[4,4,27]{2,1,0:T(4,128)S(1)}, s32[4,4,27]{2,1,0:T(4,128)}, u32[]{:S(2)}) copy-start(s32[4,4,27]{2,1,0:T(4,128)} %get-tuple-element.330) | copy-start | bytes 5188
  265.8 20.3 %copy-start.17 = (pred[4,4,27]{2,1,0:T(4,128)(4,1)S(1)}, pred[4,4,27]{2,1,0:T(4,128)(4,1)}, u32[]{:S(2)}) copy-start(pred[4,4,27]{2,1,0:T(4,128)(4,1)} %get-tuple-element.327) | copy-start | bytes 1300
  265.8 20.3 %copy-start.19 = (s32[16]{0:T(128)S(1)}, s32[16]{0:T(128)}, u32[]{:S(2)}) copy-start(s32[16]{0:T(128)} %get-tuple-element.346) | copy-start | bytes 196
  265.9 20.3 %copy-start.20 = (s32[16]{0:T(128)S(1)}, s32[16]{0:T(128)}, u32[]{:S(2)}) copy-start(s32[16]{0:T(128)} %get-tuple-element.347) | copy-start | bytes 196
  286.0 31.1 %copy-start.2 = (bf16[4,4,256,256]{3,2,1,0:T(8,128)(2,1)S(1)}, bf16[4,4,256,256]{3,2,1,0:T(8,128)(2,1)}, u32[]{:S(2)}) copy-start(bf16[4,4,256,256]{3,2,1,0:T(8,128)(2,1)} %param.17) | copy-start | bytes 6291460
  286.2 17.9 %collective-permute-start.17 = (bf16[256,256]{0,1:T(8,128)(2,1)S(1)}, bf16[256,256]{0,1:T(8,128)(2,1)S(1)}, u32[]{:S(2)}, u32[]{:S(2)}) collective-permute-start(bf16[256,256]{0,1:T(8,128)(2,1)S(1)} %bitcast.747), channel_id=1, source_target_pairs={{48,0},{64,16},{80,32},{96,48},{112,64},{49,1},{65,17},{81,33},{97... | collective-permute-start | bytes 393224 | tf_op jit(solution)/shard_map/ppermute | solution.py:27
  289.2 18.6 %collective-permute-start.8 = (bf16[2,2,256,256]{2,3,1,0:T(8,128)(2,1)S(1)}, bf16[2,2,256,256]{2,3,1,0:T(8,128)(2,1)S(1)}, u32[]{:S(2)}, u32[]{:S(2)}) collective-permute-start(bf16[2,2,256,256]{2,3,1,0:T(8,128)(2,1)S(1)} %reduce_sum.8), channel_id=1, source_target_pairs={{0,16},{16,32},{32,48},{48,64},{64,80},{80,96},{96,112},{1,17},{17... | collective-permute-start | bytes 1572872 | tf_op jit(solution)/shard_map/ppermute | solution.py:16
  292.6 18.2 %collective-permute-start.9 = (bf16[2,2,256,256]{2,3,1,0:T(8,128)(2,1)S(1)}, bf16[2,2,256,256]{2,3,1,0:T(8,128)(2,1)S(1)}, u32[]{:S(2)}, u32[]{:S(2)}) collective-permute-start(bf16[2,2,256,256]{2,3,1,0:T(8,128)(2,1)S(1)} %reduce_sum.8), channel_id=1, source_target_pairs={{16,0},{32,16},{48,32},{64,48},{80,64},{96,80},{112,96},{17,1},{33... | collective-permute-start | bytes 1572872 | tf_op jit(solution)/shard_map/ppermute | solution.py:19
  296.7 18.4 %collective-permute-start = (bf16[1,4,256,256]{3,2,1,0:T(8,128)(2,1)}, bf16[1,4,256,256]{3,2,1,0:T(8,128)(2,1)S(1)}, u32[]{:S(2)}, u32[]{:S(2)}) collective-permute-start(bf16[1,4,256,256]{3,2,1,0:T(8,128)(2,1)} %get-tuple-element.324), channel_id=1, source_target_pairs={{0,16},{16,32},{32,48},{48,64},{64,80},{80,96},{96,112},{1,17},{17... | collective-permute-start | bytes 1572872 | tf_op jit(solution)/shard_map/ppermute | solution.py:16
  300.8 16.4 %collective-permute-start.1 = (bf16[1,4,256,256]{3,2,1,0:T(8,128)(2,1)}, bf16[1,4,256,256]{3,2,1,0:T(8,128)(2,1)S(1)}, u32[]{:S(2)}, u32[]{:S(2)}) collective-permute-start(bf16[1,4,256,256]{3,2,1,0:T(8,128)(2,1)} %get-tuple-element.323), channel_id=1, source_target_pairs={{16,0},{32,16},{48,32},{64,48},{80,64},{96,80},{112,96},{17,1},{33... | collective-permute-start | bytes 1572872 | tf_op jit(solution)/shard_map/ppermute | solution.py:19
  304.1 45.7 %collective-permute-start.18 = (bf16[7,256,256]{1,2,0:T(8,128)(2,1)S(1)}, bf16[7,256,256]{1,2,0:T(8,128)(2,1)S(1)}, u32[]{:S(2)}, u32[]{:S(2)}) collective-permute-start(bf16[7,256,256]{1,2,0:T(8,128)(2,1)S(1)} %constant_dynamic-update-slice_fusion.141), channel_id=1, source_target_pairs={{0,3},{1,4},{2,5},{3,6},{4,7},{5,8},{6,9},{7,10},{8,11},{9,12},{10... | collective-permute-start | bytes 2752520 | tf_op jit(solution)/shard_map/ppermute | solution.py:27
  307.9 7.2 copy-start.6
  307.9 154.1 %collective-permute-start.4 = (bf16[2,4,256,256]{3,2,1,0:T(8,128)(2,1)}, bf16[2,4,256,256]{3,2,1,0:T(8,128)(2,1)}, u32[]{:S(2)}, u32[]{:S(2)}) collective-permute-start(bf16[2,4,256,256]{3,2,1,0:T(8,128)(2,1)} %get-tuple-element.321), channel_id=1, source_target_pairs={{0,16},{16,32},{32,48},{48,64},{64,80},{80,96},{96,112},{1,17},{17... | collective-permute-start | bytes 3145736 | tf_op jit(solution)/shard_map/ppermute | solution.py:16
  310.8 4.3 copy-start.7
  310.8 153.1 %collective-permute-start.5 = (bf16[2,4,256,256]{3,2,1,0:T(8,128)(2,1)}, bf16[2,4,256,256]{3,2,1,0:T(8,128)(2,1)}, u32[]{:S(2)}, u32[]{:S(2)}) collective-permute-start(bf16[2,4,256,256]{3,2,1,0:T(8,128)(2,1)} %get-tuple-element.322), channel_id=1, source_target_pairs={{16,0},{32,16},{48,32},{64,48},{80,64},{96,80},{112,96},{17,1},{33... | collective-permute-start | bytes 3145736 | tf_op jit(solution)/shard_map/ppermute | solution.py:19
  315.1 37.7 %collective-permute-start.19 = (bf16[7,256,256]{1,2,0:T(8,128)(2,1)S(1)}, bf16[7,256,256]{1,2,0:T(8,128)(2,1)S(1)}, u32[]{:S(2)}, u32[]{:S(2)}) collective-permute-start(bf16[7,256,256]{1,2,0:T(8,128)(2,1)S(1)} %constant_dynamic-update-slice_fusion.141), channel_id=1, source_target_pairs={{0,2},{1,3},{2,4},{3,5},{4,6},{5,7},{6,8},{7,9},{8,10},{9,11},{10,... | collective-permute-start | bytes 2752520 | tf_op jit(solution)/shard_map/ppermute | solution.py:27
  317.3 56.9 %collective-permute-start.20 = (bf16[7,256,256]{1,2,0:T(8,128)(2,1)S(1)}, bf16[7,256,256]{1,2,0:T(8,128)(2,1)S(1)}, u32[]{:S(2)}, u32[]{:S(2)}) collective-permute-start(bf16[7,256,256]{1,2,0:T(8,128)(2,1)S(1)} %constant_dynamic-update-slice_fusion.141), channel_id=1, source_target_pairs={{0,1},{1,2},{2,3},{3,4},{4,5},{5,6},{6,7},{7,8},{8,9},{9,10},{10,1... | collective-permute-start | bytes 2752520 | tf_op jit(solution)/shard_map/ppermute | solution.py:27
  322.1 111.7 %copy-start.3 = (bf16[6,4,256,256]{3,2,1,0:T(8,128)(2,1)}, bf16[6,4,256,256]{3,2,1,0:T(8,128)(2,1)S(1)}, u32[]{:S(2)}) copy-start(bf16[6,4,256,256]{3,2,1,0:T(8,128)(2,1)S(1)} %constant_dynamic-update-slice_fusion) | copy-start | bytes 9437188
  349.8 46.1 %collective-permute-start.21 = (bf16[7,256,256]{1,2,0:T(8,128)(2,1)S(1)}, bf16[7,256,256]{1,2,0:T(8,128)(2,1)S(1)}, u32[]{:S(2)}, u32[]{:S(2)}) collective-permute-start(bf16[7,256,256]{1,2,0:T(8,128)(2,1)S(1)} %constant_dynamic-update-slice_fusion.141), channel_id=1, source_target_pairs={{1,0},{2,1},{3,2},{4,3},{5,4},{6,5},{7,6},{8,7},{9,8},{10,9},{11,1... | collective-permute-start | bytes 2752520 | tf_op jit(solution)/shard_map/ppermute | solution.py:27
  352.7 46.0 %collective-permute-start.22 = (bf16[7,256,256]{1,2,0:T(8,128)(2,1)S(1)}, bf16[7,256,256]{1,2,0:T(8,128)(2,1)S(1)}, u32[]{:S(2)}, u32[]{:S(2)}) collective-permute-start(bf16[7,256,256]{1,2,0:T(8,128)(2,1)S(1)} %constant_dynamic-update-slice_fusion.141), channel_id=1, source_target_pairs={{2,0},{3,1},{4,2},{5,3},{6,4},{7,5},{8,6},{9,7},{10,8},{11,9},{12,... | collective-permute-start | bytes 2752520 | tf_op jit(solution)/shard_map/ppermute | solution.py:27
  374.1 66.3 %collective-permute-start.23 = (bf16[7,256,256]{1,2,0:T(8,128)(2,1)S(1)}, bf16[7,256,256]{1,2,0:T(8,128)(2,1)S(1)}, u32[]{:S(2)}, u32[]{:S(2)}) collective-permute-start(bf16[7,256,256]{1,2,0:T(8,128)(2,1)S(1)} %constant_dynamic-update-slice_fusion.141), channel_id=1, source_target_pairs={{3,0},{4,1},{5,2},{6,3},{7,4},{8,5},{9,6},{10,7},{11,8},{12,9},{13... | collective-permute-start | bytes 2752520 | tf_op jit(solution)/shard_map/ppermute | solution.py:27
  395.9 219.7 %collective-permute-start.10 = (bf16[6,2,256,256]{2,3,1,0:T(8,128)(2,1)}, bf16[6,2,256,256]{2,3,1,0:T(8,128)(2,1)}, u32[]{:S(2)}, u32[]{:S(2)}) collective-permute-start(bf16[6,2,256,256]{2,3,1,0:T(8,128)(2,1)} %pad_maximum_fusion.4), channel_id=1, source_target_pairs={{0,1},{1,2},{2,3},{3,4},{4,5},{5,6},{6,7},{7,8},{8,9},{9,10},{10,1... | collective-permute-start | bytes 4718600 | tf_op jit(solution)/shard_map/ppermute | solution.py:16
  398.8 216.8 %collective-permute-start.11 = (bf16[6,2,256,256]{2,3,1,0:T(8,128)(2,1)}, bf16[6,2,256,256]{2,3,1,0:T(8,128)(2,1)}, u32[]{:S(2)}, u32[]{:S(2)}) collective-permute-start(bf16[6,2,256,256]{2,3,1,0:T(8,128)(2,1)} %pad_maximum_fusion.4), channel_id=1, source_target_pairs={{1,0},{2,1},{3,2},{4,3},{5,4},{6,5},{7,6},{8,7},{9,8},{10,9},{11,1... | collective-permute-start | bytes 4718600 | tf_op jit(solution)/shard_map/ppermute | solution.py:19
  440.5 44.6 %collective-permute-start.2 = (bf16[6,1,256,256]{3,2,1,0:T(8,128)(2,1)}, bf16[6,1,256,256]{3,2,1,0:T(8,128)(2,1)S(1)}, u32[]{:S(2)}, u32[]{:S(2)}) collective-permute-start(bf16[6,1,256,256]{3,2,1,0:T(8,128)(2,1)} %get-tuple-element.319), channel_id=1, source_target_pairs={{0,1},{1,2},{2,3},{3,4},{4,5},{5,6},{6,7},{7,8},{8,9},{9,10},{10,1... | collective-permute-start | bytes 2359304 | tf_op jit(solution)/shard_map/ppermute | solution.py:16
  462.0 37.3 %collective-permute-start.3 = (bf16[6,1,256,256]{3,2,1,0:T(8,128)(2,1)}, bf16[6,1,256,256]{3,2,1,0:T(8,128)(2,1)}, u32[]{:S(2)}, u32[]{:S(2)}) collective-permute-start(bf16[6,1,256,256]{3,2,1,0:T(8,128)(2,1)} %get-tuple-element.320), channel_id=1, source_target_pairs={{1,0},{2,1},{3,2},{4,3},{5,4},{6,5},{7,6},{8,7},{9,8},{10,9},{11,1... | collective-permute-start | bytes 2359304 | tf_op jit(solution)/shard_map/ppermute | solution.py:19
  468.8 231.9 %collective-permute-start.6 = (bf16[8,2,256,256]{3,2,1,0:T(8,128)(2,1)}, bf16[8,2,256,256]{3,2,1,0:T(8,128)(2,1)}, u32[]{:S(2)}, u32[]{:S(2)}) collective-permute-start(bf16[8,2,256,256]{3,2,1,0:T(8,128)(2,1)} %get-tuple-element.317), channel_id=1, source_target_pairs={{0,1},{1,2},{2,3},{3,4},{4,5},{5,6},{6,7},{7,8},{8,9},{9,10},{10,1... | collective-permute-start | bytes 6291464 | tf_op jit(solution)/shard_map/ppermute | solution.py:16
  480.3 19.1 %copy-start.4 = (bf16[6,4,256,256]{3,2,1,0:T(8,128)(2,1)S(1)}, bf16[6,4,256,256]{3,2,1,0:T(8,128)(2,1)}, u32[]{:S(2)}) copy-start(bf16[6,4,256,256]{3,2,1,0:T(8,128)(2,1)} %copy-done.3) | copy-start | bytes 9437188
  485.1 215.6 %collective-permute-start.7 = (bf16[8,2,256,256]{3,2,1,0:T(8,128)(2,1)}, bf16[8,2,256,256]{3,2,1,0:T(8,128)(2,1)}, u32[]{:S(2)}, u32[]{:S(2)}) collective-permute-start(bf16[8,2,256,256]{3,2,1,0:T(8,128)(2,1)} %get-tuple-element.318), channel_id=1, source_target_pairs={{1,0},{2,1},{3,2},{4,3},{5,4},{6,5},{7,6},{8,7},{9,8},{10,9},{11,1... | collective-permute-start | bytes 6291464 | tf_op jit(solution)/shard_map/ppermute | solution.py:19
  621.0 6.7 copy-start.26
  627.7 63.7 %copy-start.9 = (bf16[2,2,256,256]{3,2,1,0:T(8,128)(2,1)S(1)}, bf16[2,2,256,256]{3,2,1,0:T(8,128)(2,1)}, u32[]{:S(2)}) copy-start(bf16[2,2,256,256]{3,2,1,0:T(8,128)(2,1)} %param.20) | copy-start | bytes 1572868
where the time goes:
time: 1000 us; the launch traced here: 994 us
  local copies, waits for them, and re-layouts  612 us (61%)
  matrix products  165 us (16%)
  starting transfers between devices  106 us (11%)
  waiting for transfers between devices  79.8 us (8%)
  other arithmetic  29.5 us (3%)
    unnamed x164, local copies, waits for them, and re-layouts  148 us
    gather x21, local copies, waits for them, and re-layouts, one_cell(): flattened[places]  121 us
    gather x21, local copies, waits for them, and re-layouts, one_cell(): couple_table[kind_here]  116 us
    dot_general x21, matrix products, one_cell(): jnp.einsum('jrs,jsc->rc', matrices, flattened[places], preferred_element_...  105 us
    another operation x65, local copies, waits for them, and re-layouts, coupling_table(): return jnp.stack(pieces)  104 us
    ppermute x12, waiting for transfers between devices, passed_along(): return lax.ppermute(x, axis, pairs)  67.4 us
    gather x16, local copies, waits for them, and re-layouts, one_leaf(): flattened[places]  47.3 us
    ppermute x6, starting transfers between devices, padded(): lax.ppermute(lax.slice_in_dim(block, 0, width, axis=dim), axis, backward)  46.2 us
  transfers between devices with their start and end apart: 24, of which 5 were waited for; matrix products, arithmetic and copies ran while one was open for 51% of the time, Pallas kernels for 0%

commit v1 on v0

v1 whole, which is shorter than its diff:
```python
import jax
import jax.numpy as jnp
from jax import lax
from jax.experimental import pallas as pl
from jax.experimental.pallas import tpu as pltpu
from jax.sharding import PartitionSpec as P

MESH = pl.DeviceIdType.MESH
bf16 = jnp.bfloat16
f32 = jnp.float32
LOG2E = 1.4426950408889634
LN2 = 0.6931471805599453
ROOT3 = 1.7320508075688772

HALF_INDEX = {}
for _u in range(0, 4):
    for _v in range(-3, 4):
        if max(abs(_u), abs(_v)) >= 2 and (_u > 0 or _v > 0):
            HALF_INDEX[(_u, _v)] = len(HALF_INDEX)


def nn(a, b):
    return jnp.dot(a, b, preferred_element_type=f32)


def nt(a, b):
    return lax.dot_general(a, b, (((1,), (1,)), ((), ())), preferred_element_type=f32)


def coupled(x, coup, level, u, v):
    if (u, v) in HALF_INDEX:
        return nt(x, coup[level, HALF_INDEX[(u, v)]])
    return nn(x, coup[level, HALF_INDEX[(-u, -v)]])


def far_pair(u, v):
    return max(abs(u), abs(v)) >= 2


def kernel(
    gx0,
    gy0,
    positions,
    samples,
    leaf_basis,
    transfer_one,
    transfer_two,
    couplings,
    near_lists,
    far_zero,
    far_one,
    far_two,
    out,
    basis,
    tone,
    ttwo,
    coup,
    pos,
    ext_s,
    ext_zero,
    ext_one,
    ext_two,
    field_zero,
    field_one,
    near_sum,
    part_zero,
    got_zero,
    part_one,
    got_one,
    part_two,
    got_two,
    part_near,
    got_near,
    mask_zero,
    mask_one,
    mask_two,
    own_two,
    mask_near,
    tiles,
    col_a,
    col_b,
    down_zero,
    staged,
    load_sem,
    pos_sem,
    out_sem,
    send,
    recv,
):
    X = lax.axis_index("qx")
    Y = lax.axis_index("qy")
    nx, ny = gx0 // 4, gy0 // 4
    px, py = lax.rem(X, 2), lax.rem(Y, 2)

    def at_x(k):
        return (lax.rem(X - px - 2 + k + nx, nx), Y)

    def at_y(k):
        return (X, lax.rem(Y - py - 2 + k + ny, ny))

    up, down = (lax.rem(X + nx - 1, nx), Y), (lax.rem(X + 1, nx), Y)
    left, right = (X, lax.rem(Y + ny - 1, ny)), (X, lax.rem(Y + 1, ny))

    def load(src, dst, n):
        return pltpu.make_async_copy(src, dst, load_sem.at[n])

    s_loads = [load(samples.at[r], ext_s.at[r, pl.ds(1, 4)], r) for r in range(4)]
    l_loads = [load(leaf_basis.at[r], basis.at[r], 4 + r) for r in range(4)]
    t_loads = [load(transfer_one, tone, 8), load(transfer_two, ttwo, 9)]
    c_loads = [load(couplings.at[l], coup.at[l], 10 + l) for l in range(3)]
    for r in range(4):
        s_loads[r].start()
        l_loads[r].start()

    def pos_copy(n):
        i, j = n // 6, lax.rem(n, 6)
        row = lax.rem(4 * X - 1 + i + gx0, gx0)
        col = lax.rem(4 * Y - 1 + j + gy0, gy0)
        return pltpu.make_async_copy(positions.at[row, col], pos.at[n], pos_sem.at[n])

    def start_pos(n, c):
        pos_copy(n).start()
        return c

    barrier = pltpu.get_barrier_semaphore()
    for k in range(6):

        @pl.when(k != 2 + px)
        def _():
            pl.semaphore_signal(barrier, inc=1, device_id=at_x(k), device_id_type=MESH)

        @pl.when(k != 2 + py)
        def _():
            pl.semaphore_signal(barrier, inc=1, device_id=at_y(k), device_id_type=MESH)

    for c in t_loads + c_loads:
        c.start()
    lax.fori_loop(0, 36, start_pos, 0)

    def mask_of(lst, row0, col0, rows, grid_rows, grid_cols, width):
        k = lax.broadcasted_iota(jnp.int32, (rows, 1), 0)
        b = k & 7
        r, c = row0 + (k >> 3), col0 + b
        ok = (r >= 0) & (r < grid_rows) & (c >= 0) & (c < grid_cols) & (b < width)
        ident = jnp.where(ok, r * grid_cols + c, -2)
        hit = jnp.max(jnp.where(ident == lst, 1.0, 0.0), axis=1, keepdims=True)
        return jnp.broadcast_to(hit, (rows, 128))

    for i in range(4):
        for j in range(4):
            r0, c0 = 4 * X + 2 * (i // 2) - 2, 4 * Y + 2 * (j // 2) - 2
            mask_zero[i + 2, j] = mask_of(far_zero[i, j : j + 1, :], r0, c0, 48, gx0, gy0, 6)
            mask_near[i + 1, j] = mask_of(
                near_lists[i, j : j + 1, :], 4 * X + i - 1, 4 * Y + j - 1, 24, gx0, gy0, 3
            )
    for i in range(2):
        for j in range(2):
            mask_one[i + 2, j] = mask_of(
                far_one[i, j : j + 1, :], 2 * X - 2, 2 * Y - 2, 48, gx0 // 2, gy0 // 2, 6
            )
    own_two[...] = mask_of(
        far_two[0, 0:1, :], X - px - 2, Y - py - 2, 48, gx0 // 4, gy0 // 4, 6
    )

    pl.semaphore_wait(barrier, 10)

    def remote(src, dst, n, dev):
        return pltpu.make_async_remote_copy(
            src_ref=src,
            dst_ref=dst,
            send_sem=send.at[n],
            recv_sem=recv.at[n],
            device_id=dev,
            device_id_type=MESH,
        )

    x_samples = [
        remote(samples.at[:, 3], ext_s.at[:, 0], 0, right),
        remote(samples.at[:, 0], ext_s.at[:, 5], 1, left),
    ]
    rows_lo, rows_hi = pl.ds(0, 16), pl.ds(32, 16)
    x_masks = [
        remote(mask_zero.at[pl.ds(4, 2), :, rows_hi], mask_zero.at[pl.ds(0, 2), :, rows_hi], 2, down),
        remote(mask_zero.at[pl.ds(2, 2), :, rows_lo], mask_zero.at[pl.ds(6, 2), :, rows_lo], 3, up),
        remote(mask_one.at[pl.ds(2, 2), :, rows_hi], mask_one.at[pl.ds(0, 2), :, rows_hi], 4, down),
        remote(mask_one.at[pl.ds(2, 2), :, rows_lo], mask_one.at[pl.ds(4, 2), :, rows_lo], 5, up),
        remote(mask_near.at[4, :, pl.ds(16, 8)], mask_near.at[0, :, pl.ds(16, 8)], 6, down),
        remote(mask_near.at[1, :, pl.ds(0, 8)], mask_near.at[5, :, pl.ds(0, 8)], 7, up),
    ]
    for c in x_samples + x_masks:
        c.start()

    def x_mask_two(k):
        slot = px + 4 - 2 * (k // 2)
        return pltpu.make_async_remote_copy(
            src_ref=own_two.at[pl.ds(8 * k, 8)],
            dst_ref=mask_two.at[slot],
            send_sem=send.at[40 + k],
            recv_sem=recv.at[40 + slot],
            device_id=at_x(k),
            device_id_type=MESH,
        )

    def x_two(k):
        slot = py + 4 - 2 * (k // 2)
        return pltpu.make_async_remote_copy(
            src_ref=ext_two.at[2 + py],
            dst_ref=ext_two.at[slot],
            send_sem=send.at[46 + k],
            recv_sem=recv.at[46 + slot],
            device_id=at_y(k),
            device_id_type=MESH,
        )

    def x_part_two(k):
        slot = px + 4 - 2 * (k // 2)
        return pltpu.make_async_remote_copy(
            src_ref=part_two.at[k],
            dst_ref=got_two.at[slot],
            send_sem=send.at[52 + k],
            recv_sem=recv.at[52 + slot],
            device_id=at_x(k),
            device_id_type=MESH,
        )

    def recv_wait(dst, n):
        pltpu.make_async_copy(dst, dst, recv.at[n]).wait()

    for k in range(6):

        @pl.when(k != 2 + px)
        def _():
            x_mask_two(k).start()

    mask_two[2 + px] = own_two[pl.ds(pl.multiple_of(8 * (2 + px), 8), 8), :]

    x_zero = []
    for r in range(4):
        s_loads[r].wait()
        l_loads[r].wait()
        for j in range(4):
            ext_zero[r, 2 + j] = nn(ext_s[r, 1 + j].T, basis[r, j]).astype(bf16)
        x_zero.append(
            remote(ext_zero.at[r, pl.ds(4, 2)], ext_zero.at[r, pl.ds(0, 2)], 8 + 2 * r, right)
        )
        x_zero.append(
            remote(ext_zero.at[r, pl.ds(2, 2)], ext_zero.at[r, pl.ds(6, 2)], 9 + 2 * r, left)
        )
        x_zero[-2].start()
        x_zero[-1].start()

    t_loads[0].wait()
    x_one = []
    for i in range(2):
        for j in range(2):
            total = None
            for a in range(2):
                for b in range(2):
                    term = nn(ext_zero[2 * i + a, 2 + 2 * j + b], tone[2 * i + a, 2 * j + b])
                    total = term if total is None else total + term
            ext_one[i, 2 + j] = total.astype(bf16)
        x_one.append(remote(ext_one.at[i, pl.ds(2, 2)], ext_one.at[i, pl.ds(0, 2)], 16 + 2 * i, right))
        x_one.append(remote(ext_one.at[i, pl.ds(2, 2)], ext_one.at[i, pl.ds(4, 2)], 17 + 2 * i, left))
        x_one[-2].start()
        x_one[-1].start()

    t_loads[1].wait()
    total = None
    for a in range(2):
        for b in range(2):
            term = nn(ext_one[a, 2 + b], ttwo[a, b])
            total = term if total is None else total + term
    ext_two[2 + py] = total.astype(bf16)
    for k in range(6):

        @pl.when(k != 2 + py)
        def _():
            x_two(k).start()

    def wait_pos(n, c):
        pos_copy(n).wait()
        return c

    lax.fori_loop(0, 36, wait_pos, 0)
    pos[...] = pos[...] * (ROOT3 * LOG2E)

    def near_target(i, j, first, count, store):
        here = pos[i * 6 + j + 1]
        col_a[...] = jnp.broadcast_to(here[0:1], (128, 256)).T
        col_b[...] = jnp.broadcast_to(here[1:2], (128, 256)).T
        for q in range(count):
            for b in range(3):
                sr = first + q
                there = pos[(sr + 1) * 6 + j + b]
                xs, ys = there[0:1], there[1:2]
                mask = mask_near[i, j, pl.ds((sr - i + 2) * 8 + b, 1), :]
                c0, c1 = mask * 0.0625, mask * (0.0625 * LN2)
                for h in range(2):
                    lanes = slice(128 * h, 128 * h + 128)
                    for w in range(8):
                        span = slice(32 * w, 32 * w + 32)
                        dx = col_a[span, :] - xs[:, lanes]
                        dy = col_b[span, :] - ys[:, lanes]
                        d2 = jnp.maximum(dx * dx + dy * dy, 1e-30)
                        d = d2 * lax.rsqrt(d2)
                        value = (c0 + c1 * d) * jnp.exp2(-d)
                        tiles[q * 3 + b, span, lanes] = value.astype(bf16)
        total = None
        for q in range(count):
            for b in range(3):
                term = nn(tiles[q * 3 + b], ext_s[first + q, j + b])
                total = term if total is None else total + term
        store(total)

    def near_columns(column):
        def middle(n, c):
            i, j = n // 2, column(lax.rem(n, 2))

            def store(v):
                near_sum[i + 1, j] = v

            near_target(i + 2, j, i, 3, store)
            return c

        def edge(n, c):
            e, j = n // 2, column(lax.rem(n, 2))

            def store(v):
                near_sum[3 * e, j] = v

            near_target(3 * e + 1, j, 2 * e, 2, store)
            return c

        def outer(n, c):
            e, j = n // 2, column(lax.rem(n, 2))

            def store(v):
                part_near[e, j] = v.astype(bf16)

            near_target(5 * e, j, 3 * e, 1, store)
            return c

        lax.fori_loop(0, 4, outer, 0)
        lax.fori_loop(0, 4, middle, 0)
        lax.fori_loop(0, 4, edge, 0)

    for c in x_masks:
        c.wait()
    near_columns(lambda q: q + 1)
    for c in x_samples:
        c.wait()
    near_columns(lambda q: 3 * q)
    x_near = [
        remote(part_near.at[0], got_near.at[1], 20, up),
        remote(part_near.at[1], got_near.at[0], 21, down),
    ]
    for c in x_near:
        c.start()

    for c in c_loads:
        c.wait()
    for c in x_zero:
        c.wait()

    def far_zero_row(i):
        if i < 0:
            rows, shift = (0, 1), 4
        elif i > 3:
            rows, shift = (2, 3), -2
        else:
            rows, shift = (0, 1, 2, 3), (2 if i < 2 else 0)
        for p in range(2):

            def body(h, c):
                j = 2 * h + p
                total = None
                for sr in rows:
                    for b in range(6):
                        u, v = sr - i, b - 2 - p
                        if not far_pair(u, v):
                            continue
                        m = mask_zero[i + 2, j, pl.ds((sr + shift) * 8 + b, 1), :]
                        m = jnp.concatenate([m, m], axis=1).astype(bf16)
                        term = coupled(ext_zero[sr, 2 * h + b] * m, coup, 0, u, v)
                        total = term if total is None else total + term
                if i < 0:
                    part_zero[i + 2, j] = total.astype(bf16)
                elif i > 3:
                    part_zero[i - 2, j] = total.astype(bf16)
                else:
                    field_zero[i, j] = total
                return c

            lax.fori_loop(0, 2, body, 0)

    far_zero_row(-2)
    far_zero_row(-1)
    x_far = [remote(part_zero.at[pl.ds(0, 2)], got_zero.at[pl.ds(2, 2)], 22, up)]
    x_far[0].start()
    far_zero_row(4)
    far_zero_row(5)
    x_far.append(remote(part_zero.at[pl.ds(2, 2)], got_zero.at[pl.ds(0, 2)], 23, down))
    x_far[1].start()
    for i in range(4):
        far_zero_row(i)

    for c in x_one:
        c.wait()

    def far_one_row(i):
        for j in range(2):
            total = None
            for sr in range(2):
                for b in range(6):
                    u, v = sr - i, b - 2 - j
                    if not far_pair(u, v):
                        continue
                    a = sr + 2 if 0 <= i < 2 else (sr + 4 if i < 0 else sr)
                    m = mask_one[i + 2, j, pl.ds(a * 8 + b, 1), :]
                    m = jnp.concatenate([m, m], axis=1).astype(bf16)
                    term = coupled(ext_one[sr, b] * m, coup, 1, u, v)
                    total = term if total is None else total + term
            if i < 0:
                part_one[0, i + 2, j] = total.astype(bf16)
            elif i > 1:
                part_one[1, i - 2, j] = total.astype(bf16)
            else:
                field_one[i, j] = total

    far_one_row(-2)
    far_one_row(-1)
    x_far.append(remote(part_one.at[0], got_one.at[1], 24, up))
    x_far[2].start()
    far_one_row(2)
    far_one_row(3)
    x_far.append(remote(part_one.at[1], got_one.at[0], 25, down))
    x_far[3].start()

    for k in range(6):

        @pl.when(k != 2 + py)
        def _():
            x_two(k).wait_send()
            recv_wait(ext_two.at[k], 46 + k)

        @pl.when(k != 2 + px)
        def _():
            x_mask_two(k).wait_send()
            recv_wait(mask_two.at[k], 40 + k)

    for qx in range(2):
        for qy in range(2):

            @pl.when((px == qx) & (py == qy))
            def _():
                for k in range(6):
                    u = qx + 2 - k
                    total = None
                    for b in range(6):
                        v = b - 2 - qy
                        if not far_pair(u, v):
                            continue
                        m = mask_two[k, pl.ds(b, 1), :]
                        m = jnp.concatenate([m, m], axis=1).astype(bf16)
                        term = coupled(ext_two[b] * m, coup, 2, u, v)
                        total = term if total is None else total + term
                    part_two[k] = total.astype(bf16)

    for k in range(6):

        @pl.when(k != 2 + px)
        def _():
            x_part_two(k).start()

    far_one_row(0)
    far_one_row(1)

    for k in range(6):

        @pl.when(k != 2 + px)
        def _():
            x_part_two(k).wait_send()
            recv_wait(got_two.at[k], 52 + k)

    got_two[2 + px] = part_two[2 + px]
    total = got_two[0].astype(f32)
    for k in range(1, 6):
        total += got_two[k].astype(f32)
    down_two = total.astype(bf16)
    for c in x_far:
        c.wait()
    for c in x_near:
        c.wait()
    down_one = []
    for i in range(2):
        for j in range(2):
            value = field_one[i, j] + nt(down_two, ttwo[i, j])
            value += got_one[0, i, j].astype(f32) + got_one[1, i, j].astype(f32)
            part_one[0, i, j] = value.astype(bf16)

    def descend(n, c):
        i, h = n // 2, lax.rem(n, 2)
        for b in range(2):
            j = 2 * h + b
            value = field_zero[i, j] + nt(part_one[0, i // 2, h], tone[i, j])
            down_zero[i, j] = (value + got_zero[i, j].astype(f32)).astype(bf16)
        return c

    lax.fori_loop(0, 8, descend, 0)

    for e in range(2):
        for j in range(4):
            near_sum[3 * e, j] += got_near[e, j].astype(f32)

    def finish(i, c):
        for j in range(4):
            staged[i, j] = (near_sum[i, j] + nt(basis[i, j], down_zero[i, j])).astype(bf16)
        pltpu.make_async_copy(staged.at[i], out.at[i], out_sem.at[i]).start()
        return c

    lax.fori_loop(0, 4, finish, 0)

    def drain(i, c):
        pltpu.make_async_copy(staged.at[i], out.at[i], out_sem.at[i]).wait()
        return c

    lax.fori_loop(0, 4, drain, 0)


def solution(mesh):
    nx, ny = mesh.shape["qx"], mesh.shape["qy"]

    def per_device(
        positions,
        samples,
        leaf_basis,
        transfer_one,
        transfer_two,
        couplings,
        near_lists,
        far_zero,
        far_one,
        far_two,
    ):
        def body(*refs):
            kernel(4 * nx, 4 * ny, *refs)

        hbm = pl.BlockSpec(memory_space=pl.ANY)
        vmem = pl.BlockSpec(memory_space=pltpu.VMEM)
        block = (256, 256)
        return pl.pallas_call(
            body,
            out_shape=jax.ShapeDtypeStruct(samples.shape, bf16),
            in_specs=[hbm] * 6 + [vmem] * 4,
            out_specs=hbm,
            scratch_shapes=[
                pltpu.VMEM((4, 4) + block, bf16),
                pltpu.VMEM((4, 4) + block, bf16),
                pltpu.VMEM((2, 2) + block, bf16),
                pltpu.VMEM((3, 20) + block, bf16),
                pltpu.VMEM((36, 2, 256), f32),
                pltpu.VMEM((4, 6) + block, bf16),
                pltpu.VMEM((4, 8) + block, bf16),
                pltpu.VMEM((2, 6) + block, bf16),
                pltpu.VMEM((6,) + block, bf16),
                pltpu.VMEM((4, 4) + block, f32),
                pltpu.VMEM((2, 2) + block, f32),
                pltpu.VMEM((4, 4) + block, f32),
                pltpu.VMEM((4, 4) + block, bf16),
                pltpu.VMEM((4, 4) + block, bf16),
                pltpu.VMEM((2, 2, 2) + block, bf16),
                pltpu.VMEM((2, 2, 2) + block, bf16),
                pltpu.VMEM((6,) + block, bf16),
                pltpu.VMEM((6,) + block, bf16),
                pltpu.VMEM((2, 4) + block, bf16),
                pltpu.VMEM((2, 4) + block, bf16),
                pltpu.VMEM((8, 4, 48, 128), f32),
                pltpu.VMEM((6, 2, 48, 128), f32),
                pltpu.VMEM((6, 8, 128), f32),
                pltpu.VMEM((48, 128), f32),
                pltpu.VMEM((6, 4, 24, 128), f32),
                pltpu.VMEM((9,) + block, bf16),
                pltpu.VMEM((256, 128), f32),
                pltpu.VMEM((256, 128), f32),
                pltpu.VMEM((4, 4) + block, bf16),
                pltpu.VMEM((4, 4) + block, bf16),
                pltpu.SemaphoreType.DMA((13,)),
                pltpu.SemaphoreType.DMA((36,)),
                pltpu.SemaphoreType.DMA((4,)),
                pltpu.SemaphoreType.DMA((58,)),
                pltpu.SemaphoreType.DMA((58,)),
            ],
            compiler_params=pltpu.CompilerParams(
                collective_id=0, has_side_effects=True, vmem_limit_bytes=60 << 20
            ),
        )(
            positions,
            samples,
            leaf_basis,
            transfer_one,
            transfer_two,
            couplings,
            near_lists,
            far_zero,
            far_one,
            far_two,
        )

    cell = P("qx", "qy", None, None)
    short = P("qx", "qy", None)
    return jax.shard_map(
        per_device,
        mesh=mesh,
        in_specs=(P(), cell, cell, cell, cell, P(), short, short, short, short),
        out_specs=cell,
        check_vma=False,
    )
```

time: 1000 us -> 95 us (0.10)
  the two profiles are of different devices: /device:TPU:116 before, /device:TPU:1 now
where the time goes in v1:
time: 95 us; the launch traced here: 94.8 us
  Pallas kernels  91.7 us (97%)
  local copies, waits for them, and re-layouts  3.1 us (3%)
    pallas_call x1, Pallas kernels, per_device(): pl.pallas_call(body, out_shape=jax.ShapeDtypeStruct(samples.shape, bf16),...  91.7 us
    unnamed x1, local copies, waits for them, and re-layouts  3.1 us

profile of v1, /device:TPU:1, one launch (start us, length us, event | category | flops | bytes accessed | tf_op | source)
XLA Modules:
  0.0 94.8 jit_solution(17072286055804994783)
XLA Ops:
  0.0 91.7 %shard_map.100 = bf16[4,4,256,256]{3,2,1,0:T(8,128)(2,1)} custom-call(f32[32,64,2,256]{3,2,1,0:T(2,128)} %refs_0_.1, bf16[4,4,256,256]{3,2,1,0:T(8,128)(2,1)} %refs_1_.1, bf16[4,4,256,256]{3,2,1,0:T(8,128)(2,1)} %refs_2_.1, bf16[4,4,256,256]{3,2,1,0:T(8,128)(2,1)} %refs_3_.1, bf16[2,2,256,256]{3,2,1,0:T(8,128)(2,1)} %refs_4_.1, ...), custom_call_target="tpu_custom_call" | custom-call | tf_op jit(solution)/shard_map/pallas_call | solution.py:551
  91.7 3.1 %copy.12 = bf16[4,4,256,256]{3,2,1,0:T(8,128)(2,1)} copy(bf16[4,4,256,256]{3,2,1,0:T(8,128)(2,1)} %shard_map.100) | data formatting | bytes 4194304
